TPU v7x, 512 devices: a whole 4x4x16 slice. The times are simulated.
512 devices in a mesh: dom: 128 (over x, y_hi, z), rel: 4 (over y_lo, core).
Axes of the slice: x: 4, y: 4 (y_hi: 2, y_lo: 2; y = y_hi * 2 + y_lo), z: 16, core: 2. Of those that a mesh axis runs over, the one named last changes fastest.
Arguments:
- emb: float32 [32768, 400], P('dom'), may hold values from -1.2 to 1.2
- emb_state: float32 [32768], P('dom'), may hold values from 0.02 to 2
- rel_weight: float32 [32, 400], P('rel'), may hold values from 0.5 to 1.5
- rel_state: float32 [32], P('rel'), may hold values from 1 to 1000
- swap_mask: int32 [1], replicated, may hold values from 1 to 127
- src_rows: int32 [4, 65536], P('rel', 'dom'), may hold values from 0 to 255
- dst_rows: int32 [4, 65536], P('rel', 'dom'), may hold values from 0 to 255
- tile_rel: int32 [4, 512], P('rel', 'dom'), may hold values from 0 to 7
- live_tiles: int32 [4, 128], P('rel', 'dom'), may hold values from 1 to 4, as said below
- neg_tiles: int32 [4, 1024], P('rel', 'dom'), may hold values from 0 to 1
- bound_rows: int32 [32768], P('dom'), may hold values from 0 to 255
- band_src: int32 [4, 32768], P('rel', 'dom'), may hold values from 0 to 255
- band_dst: int32 [4, 32768], P('rel', 'dom'), may hold values from 0 to 255
- band_rel: int32 [4, 256], P('rel', 'dom'), may hold values from 0 to 7
Outputs:
- emb_new: float32 [32768, 400], P('dom')
- state_new: float32 [32768], P('dom')
- rel_new: float32 [32, 400], P('rel')
Inputs may be any that keep to these rules, and one draw needn't show every extreme that they name: `live_tiles`: each entry counts the leading edge tiles of one bucket that hold edges; some relation group and partition has all 4 tiles live in every draw. `swap_mask`: the same plan entry holds for every partition, so pairs are mutual.
All inputs are finite; a program needn't handle non-finite values.
Results may differ from a plain program's by a relative error of at most 0.0029.
Values may be sent and summed in bfloat16 or wider, within the bound.
No kernel may reach another device: no remote copies, remote signals or barrier semaphores. Data moves between devices by JAX's collectives and lax.ppermute only.
A program may use at most 64 MiB of HBM per device.

v0:
```python
import jax
import jax.numpy as jnp
from jax import lax
from jax.sharding import PartitionSpec as P

step_rate = 0.25


def from_partner(block, axis, distance):
    count = lax.axis_size(axis)
    route = []
    for low in range(count):
        high = low | 1 << distance
        if high != low and high < count:
            route += [(low, high), (high, low)]
    return lax.ppermute(block, axis, route)


def padded_2(block, sides, width):
    for axis, dim in sides:
        count = lax.axis_size(axis)
        forward = [(i, i + 1) for i in range(count - 1)]
        backward = [(target, source) for source, target in forward]
        low = lax.ppermute(
            lax.slice_in_dim(block, block.shape[dim] - width, None, axis=dim), axis, forward
        )
        high = lax.ppermute(lax.slice_in_dim(block, 0, width, axis=dim), axis, backward)
        block = jnp.concatenate([low, block, high], axis=dim)
    return block


def edge_terms(q, target, negs, valid):
    pos = jnp.sum(q.astype(jnp.float32) * target.astype(jnp.float32), axis=1)
    neg = jnp.einsum("ed,nd->en", q, negs, preferred_element_type=jnp.float32)
    dpos = -jax.nn.sigmoid(-pos) * valid
    dneg = (jax.nn.sigmoid(neg) * (valid / negs.shape[0])[:, None]).astype(jnp.bfloat16)
    dq = dpos[:, None] * target.astype(jnp.float32) + jnp.einsum(
        "en,nd->ed", dneg, negs, preferred_element_type=jnp.float32
    )
    dtarget = dpos[:, None] * q.astype(jnp.float32)
    dnegs = jnp.einsum("en,ed->nd", dneg, q, preferred_element_type=jnp.float32)
    return (dq, dtarget, dnegs)


def bit_set(mask, bit):
    return mask // (1 << bit) % 2 == 1


def keep_same(values):
    return values


def route_block(values, mask):
    levels = lax.axis_size("dom").bit_length() - 1
    for bit in range(levels):

        def route_moved(current, level=bit):
            return from_partner(current, "dom", level)

        values = lax.cond(bit_set(mask, bit), route_moved, keep_same, values)
    return values


def return_block(values, mask):
    levels = lax.axis_size("dom").bit_length() - 1
    for bit in range(levels):

        def return_moved(current, level=bit):
            return from_partner(current, "dom", level)

        values = lax.cond(bit_set(mask, bit), return_moved, keep_same, values)
    return values


def adagrad(table, state, grad):
    fresh = state + jnp.mean(grad * grad, axis=1)
    return (table - step_rate * grad / jnp.sqrt(fresh)[:, None], fresh)


def relation_onehot(ids, count, tile):
    per_edge = jnp.repeat(ids, tile)
    return (per_edge[:, None] == jnp.arange(count)[None, :]).astype(jnp.float32)


def body(
    emb,
    emb_state,
    rel_weight,
    rel_state,
    swap_mask,
    src_rows,
    dst_rows,
    tile_rel,
    live_tiles,
    neg_tiles,
    bound_rows,
    band_src,
    band_dst,
    band_rel,
):
    part_rows, width = emb.shape
    tile = 128
    group = 4
    rel_count = rel_weight.shape[0]
    bnd = bound_rows.shape[0] // 2
    part_tiles = part_rows // tile
    neg_ids = neg_tiles[0]
    mask = swap_mask[0]
    own_bf = emb.astype(jnp.bfloat16)
    far = route_block(own_bf, mask)
    rim = own_bf[bound_rows]
    padded = padded_2(rim, (("dom", 0),), bnd)
    near = jnp.concatenate([padded[:bnd], padded[-bnd:]], axis=0)
    pick = (neg_ids[:, None] == jnp.arange(part_tiles)[None, :]).astype(jnp.float32)
    negs = jnp.einsum(
        "np,prd->nrd",
        pick.astype(jnp.bfloat16),
        far.reshape(part_tiles, tile, width),
        preferred_element_type=jnp.float32,
    )
    negs = negs.astype(jnp.bfloat16).reshape(neg_ids.shape[0] * tile, width)
    tile_ids = tile_rel[0]
    tile_onehot = (tile_ids[:, None] == jnp.arange(rel_count)[None, :]).astype(jnp.float32)
    w_tiles = jnp.dot(tile_onehot, rel_weight, precision=lax.Precision.HIGHEST)
    live = live_tiles[0, 0]
    sources = src_rows[0]
    targets = dst_rows[0]

    def run_block(index, carry):
        own_grad, far_grad, neg_grad, rel_grad = carry
        w_edge = jnp.broadcast_to(w_tiles[:, None, :], (group, tile, width)).reshape(
            group * tile, width
        )
        valid = (index * group + jnp.arange(group * tile) // tile < live).astype(jnp.float32)
        rows = emb[sources]
        q = (rows * w_edge).astype(jnp.bfloat16)
        dq, dtarget, dnegs = edge_terms(q, far[targets], negs, valid)
        own_grad = own_grad.at[sources].add(dq * w_edge)
        far_grad = far_grad.at[targets].add(dtarget)
        rel_grad = rel_grad + jnp.einsum(
            "er,ed->rd",
            relation_onehot(tile_ids, rel_count, tile),
            dq * rows,
            precision=lax.Precision.HIGHEST,
        )
        return (own_grad, far_grad, neg_grad + dnegs, rel_grad)

    start = (
        jnp.zeros((part_rows, width), jnp.float32),
        jnp.zeros((part_rows, width), jnp.float32),
        jnp.zeros(negs.shape, jnp.float32),
        jnp.zeros((rel_count, width), jnp.float32),
    )
    blocks_live = (live + group - 1) // group
    own_grad, far_grad, neg_grad, rel_grad = lax.fori_loop(0, blocks_live, run_block, start)
    band_ids = band_rel[0]
    band_tiles = band_ids.shape[0]
    band_onehot = (band_ids[:, None] == jnp.arange(rel_count)[None, :]).astype(jnp.float32)
    w_band_tiles = jnp.dot(band_onehot, rel_weight, precision=lax.Precision.HIGHEST)
    w_band = jnp.broadcast_to(w_band_tiles[:, None, :], (band_tiles, tile, width)).reshape(
        band_tiles * tile, width
    )
    band_from = band_src[0]
    band_to = band_dst[0]
    band_rows = emb[band_from]
    band_q = (band_rows * w_band).astype(jnp.bfloat16)
    band_valid = jnp.ones((band_tiles * tile,), jnp.float32)
    dq, dtarget, dnegs = edge_terms(band_q, near[band_to], negs, band_valid)
    own_grad = own_grad.at[band_from].add(dq * w_band)
    neg_grad = neg_grad + dnegs
    rel_grad = rel_grad + jnp.einsum(
        "er,ed->rd",
        relation_onehot(band_ids, rel_count, tile),
        dq * band_rows,
        precision=lax.Precision.HIGHEST,
    )
    far_grad = far_grad + jnp.einsum(
        "np,nrd->prd",
        pick,
        neg_grad.reshape(neg_ids.shape[0], tile, width),
        precision=lax.Precision.HIGHEST,
    ).reshape(part_rows, width)
    near_grad = jnp.zeros((2 * bnd, width), jnp.float32).at[band_to].add(dtarget)
    padded_grad = padded_2(near_grad.astype(jnp.bfloat16), (("dom", 0),), bnd).astype(
        near_grad.dtype
    )
    returned = jnp.concatenate([padded_grad[:bnd], padded_grad[-bnd:]], axis=0)
    local = own_grad.at[bound_rows].add(returned)
    total_rel = lax.psum(rel_grad, "dom")
    rel_new = (
        rel_weight
        - step_rate
        * total_rel
        / jnp.sqrt(rel_state + jnp.mean(total_rel * total_rel, axis=1))[:, None]
    )
    whole_grad = local + return_block(far_grad, mask)
    full_grad = lax.psum(whole_grad, "rel")
    emb_new, state_new = adagrad(emb, emb_state, full_grad)
    return (emb_new, state_new, rel_new)


def solution(mesh):
    in_specs = (
        P("dom", None),
        P("dom"),
        P("rel", None),
        P("rel"),
        P(),
        P("rel", "dom"),
        P("rel", "dom"),
        P("rel", "dom"),
        P("rel", "dom"),
        P("rel", "dom"),
        P("dom"),
        P("rel", "dom"),
        P("rel", "dom"),
        P("rel", "dom"),
    )
    out_specs = (P("dom", None), P("dom"), P("rel", None))
    return jax.shard_map(body, mesh=mesh, in_specs=in_specs, out_specs=out_specs, check_vma=False)
```

profile of v0, /device:TPU:1, one launch (start us, length us, event | category | flops | bytes accessed | tf_op | source)
XLA Modules:
  0.0 930.4 jit_solution(13966147584618793165)
XLA Ops:
  11.7 5.6 collective-permute-start.14
  18.9 7.7 conditional.14
  18.9 2.9 collective-permute-start
  21.8 4.8 collective-permute-done
  26.6 1.6 gather_fusion.2
  30.5 19.1 %conditional.15 = (bf16[256,400]{1,0:T(8,128)(2,1)}) conditional(s32[]{:T(128)} %convert_element_type.167, bf16[256,400]{1,0:T(8,128)(2,1)} %get-tuple-element.671, bf16[256,400]{1,0:T(8,128)(2,1)} %get-tuple-element.671), branch_computations={%region_2.3_spmd, %region_3.4_spmd} | conditional | bytes 1228848 | solution.py:60
  30.5 7.1 collective-permute-start.1
  37.5 11.3 %collective-permute-done.1 = bf16[256,400]{1,0:T(8,128)(2,1)S(1)} collective-permute-done((bf16[256,400]{1,0:T(8,128)(2,1)}, bf16[256,400]{1,0:T(8,128)(2,1)S(1)}, u32[]{:S(2)}, u32[]{:S(2)}) %collective-permute-start.1) | collective-permute-done | bytes 204832 | tf_op jit(solution)/shard_map/cond/branch_1_fun/ppermute | solution.py:16
  49.5 3.0 gather_fusion.3
  58.2 33.8 %while.21 = (s32[]{:T(128)}, f32[256,400]{1,0:T(8,128)S(1)}, f32[256,400]{1,0:T(8,128)S(1)}, f32[1024,400]{0,1:T(8,128)}, f32[8,400]{1,0:T(8,128)S(1)}, /*index=...) while((s32[]{:T(128)}, f32[256,400]{1,0:T(8,128)S(1)}, ...), condition=%wide.region_18.19_spmd, body=%wide.region_15.18_spmd.sunk | while | flops 1283260032 | bytes 38448668 | solution.py:155
  60.4 2.3 gather_fusion
  62.7 1.5 copy.88
  65.7 2.0 multiply_convert_fusion.3
  67.7 3.6 gather_fusion.1
  71.4 2.0 copy.89
  73.3 3.5 bitcast_multiply_fusion.6
  78.3 3.8 scatter_fusion
  83.6 3.8 scatter_fusion.1
  87.4 3.7 convolution_add_fusion.7
  98.9 1.9 gather_fusion.6
  106.8 14.5 %conditional.21 = (f32[256,400]{1,0:T(8,128)S(1)}) conditional(s32[]{:T(128)} %convert_element_type.168, f32[256,400]{1,0:T(8,128)S(1)} %bitcast_add_fusion, f32[256,400]{1,0:T(8,128)S(1)} %bitcast_add_fusion), branch_computations={%region_19.20_spmd, %region_20.21_spmd} | conditional | bytes 2457648 | solution.py:71
  106.8 3.7 collective-permute-start.7
  110.6 10.8 %collective-permute-done.7 = f32[256,400]{1,0:T(8,128)S(1)} collective-permute-done((f32[256,400]{1,0:T(8,128)S(1)}, f32[256,400]{1,0:T(8,128)S(1)}, u32[]{:S(2)}, u32[]{:S(2)}) %collective-permute-start.7) | collective-permute-done | bytes 409632 | tf_op jit(solution)/shard_map/cond/branch_1_fun/ppermute | solution.py:16
  121.4 28.7 %conditional.22 = (f32[256,400]{1,0:T(8,128)S(1)}) conditional(s32[]{:T(128)} %convert_element_type.167, f32[256,400]{1,0:T(8,128)S(1)} %get-tuple-element.678, f32[256,400]{1,0:T(8,128)S(1)} %get-tuple-element.678), branch_computations={%region_21.22_spmd, %region_22.23_spmd} | conditional | bytes 2457648 | solution.py:71
  121.4 5.9 collective-permute-start.8
  127.3 22.7 %collective-permute-done.8 = f32[256,400]{1,0:T(8,128)S(1)} collective-permute-done((f32[256,400]{1,0:T(8,128)S(1)}, f32[256,400]{1,0:T(8,128)S(1)}, u32[]{:S(2)}, u32[]{:S(2)}) %collective-permute-start.8) | collective-permute-done | bytes 409632 | tf_op jit(solution)/shard_map/cond/branch_1_fun/ppermute | solution.py:16
  152.3 2.7 scatter_custom_fusion.3
  156.4 4.6 collective-permute-start.16
  161.3 600.9 %psum.15 = f32[8,400]{1,0:T(8,128)S(1)} all-reduce(f32[8,400]{1,0:T(8,128)S(1)} %convolution_add_fusion.4), channel_id=1, replica_groups=mesh['dom'=128,'rel'=4] {'dom'}, use_global_device_ids=true, to_apply=%region_39.40 | all-reduce | flops 3200 | bytes 25600 | tf_op jit(solution)/shard_map/psum | solution.py:189
  763.4 2.3 scatter_fusion.2
  766.9 2.3 scatter_custom_fusion.4
  770.8 149.0 %all-reduce.2.cloned.1.call-done = f32[256,400]{1,0:T(8,128)} async-done(((f32[256,400]{1,0:T(8,128)}), f32[256,400]{1,0:T(8,128)}) %all-reduce.2.cloned.1.call-update) | async-done | bytes 409616 | tf_op jit(solution)/shard_map/psum | solution.py:197
  (139 shorter events, 44.5 us)
Async XLA Ops:
  7.2 1.3 copy-start.18
  7.2 912.6 %all-reduce.2.cloned.1.call-start = ((), (), s32[]{:S(2)}) async-start(), calls=%async_computation | async-start | bytes 1048576 | tf_op jit(solution)/shard_map/psum | solution.py:197
  8.5 18.0 %copy-start.14 = (s32[1,512]{1,0:T(1,128)S(1)}, s32[1,512]{1,0:T(1,128)}, u32[]{:S(2)}) copy-start(s32[1,512]{1,0:T(1,128)} %param.50) | copy-start | bytes 6148
  8.5 18.0 %copy-start.13 = (s32[1,512]{1,0:T(1,128)S(1)}, s32[1,512]{1,0:T(1,128)}, u32[]{:S(2)}) copy-start(s32[1,512]{1,0:T(1,128)} %param.49) | copy-start | bytes 6148
  10.4 87.5 %collective-permute-start.15 = (bf16[128,400]{1,0:T(8,128)(2,1)}, bf16[128,400]{1,0:T(8,128)(2,1)}, u32[]{:S(2)}, u32[]{:S(2)}) collective-permute-start(bf16[128,400]{1,0:T(8,128)(2,1)} %get-tuple-element.513), channel_id=1, source_target_pairs={{4,0},{8,4},{12,8},{16,12},{20,16},{24,20},{28,24},{32,28},{36,32}... | collective-permute-start | bytes 307208 | tf_op jit(solution)/shard_map/ppermute | solution.py:27
  11.7 86.2 %collective-permute-start.14 = (bf16[128,400]{1,0:T(8,128)(2,1)}, bf16[128,400]{1,0:T(8,128)(2,1)}, u32[]{:S(2)}, u32[]{:S(2)}) collective-permute-start(bf16[128,400]{1,0:T(8,128)(2,1)} %get-tuple-element.512), channel_id=1, source_target_pairs={{0,4},{4,8},{8,12},{12,16},{16,20},{20,24},{24,28},{28,32},{32,36}... | collective-permute-start | bytes 307208 | tf_op jit(solution)/shard_map/ppermute | solution.py:24
  18.9 7.7 collective-permute-start
  26.6 1.7 copy-start.22
  26.6 1.7 copy-start.15
  26.6 2.8 copy-start.16
  30.5 18.4 %collective-permute-start.1 = (bf16[256,400]{1,0:T(8,128)(2,1)}, bf16[256,400]{1,0:T(8,128)(2,1)S(1)}, u32[]{:S(2)}, u32[]{:S(2)}) collective-permute-start(bf16[256,400]{1,0:T(8,128)(2,1)} %param.3), channel_id=1, source_target_pairs={{0,8},{8,0},{4,12},{12,4},{16,24},{24,16},{20,28},{28,20},{32,40},... | collective-permute-start | bytes 614408 | tf_op jit(solution)/shard_map/cond/branch_1_fun/ppermute | solution.py:16
  52.5 1.4 copy-start.17
  54.3 0.9 copy-start.5
  58.2 33.8 %copy-start.19 = (s32[1,256]{1,0:T(1,128)S(1)}, s32[1,256]{1,0:T(1,128)}, u32[]{:S(2)}) copy-start(s32[1,256]{1,0:T(1,128)} %param.56) | copy-start | bytes 3076
  58.2 33.8 %copy-start.20 = (s32[1,256]{1,0:T(1,128)S(1)}, s32[1,256]{1,0:T(1,128)}, u32[]{:S(2)}) copy-start(s32[1,256]{1,0:T(1,128)} %param.55) | copy-start | bytes 3076
  64.2 1.5 copy-start.4
  65.3 2.4 copy-start.3
  87.4 3.8 copy-start
  93.1 1.9 copy-start.10
  93.1 3.4 copy-start.6
  98.9 3.5 copy-start.7
  101.9 1.0 copy-start.8
  102.9 2.0 copy-start.1
  106.8 14.5 %collective-permute-start.7 = (f32[256,400]{1,0:T(8,128)S(1)}, f32[256,400]{1,0:T(8,128)S(1)}, u32[]{:S(2)}, u32[]{:S(2)}) collective-permute-start(f32[256,400]{1,0:T(8,128)S(1)} %param.17), channel_id=1, source_target_pairs={{0,4},{4,0},{8,12},{12,8},{16,20},{20,16},{24,28},{28,24},{32,36},... | collective-permute-start | bytes 1228808 | tf_op jit(solution)/shard_map/cond/branch_1_fun/ppermute | solution.py:16
  121.4 28.6 %collective-permute-start.8 = (f32[256,400]{1,0:T(8,128)S(1)}, f32[256,400]{1,0:T(8,128)S(1)}, u32[]{:S(2)}, u32[]{:S(2)}) collective-permute-start(f32[256,400]{1,0:T(8,128)S(1)} %param.19), channel_id=1, source_target_pairs={{0,8},{8,0},{4,12},{12,4},{16,24},{24,16},{20,28},{28,20},{32,40},... | collective-permute-start | bytes 1228808 | tf_op jit(solution)/shard_map/cond/branch_1_fun/ppermute | solution.py:16
  150.1 1.1 copy-start.12
  151.3 9.7 %copy-start.11 = (f32[256,400]{0,1:T(8,128)S(1)}, f32[256,400]{0,1:T(8,128)}, u32[]{:S(2)}) copy-start(f32[256,400]{0,1:T(8,128)} %get-tuple-element.515) | copy-start | bytes 1228804
  155.1 610.8 %collective-permute-start.17 = (bf16[128,400]{1,0:T(8,128)(2,1)S(1)}, bf16[128,400]{1,0:T(8,128)(2,1)}, u32[]{:S(2)}, u32[]{:S(2)}) collective-permute-start(bf16[128,400]{1,0:T(8,128)(2,1)S(1)} %get-tuple-element.511), channel_id=1, source_target_pairs={{4,0},{8,4},{12,8},{16,12},{20,16},{24,20},{28,24},{32,28},{36,32}... | collective-permute-start | bytes 307208 | tf_op jit(solution)/shard_map/ppermute | solution.py:27
  156.4 609.5 %collective-permute-start.16 = (bf16[128,400]{1,0:T(8,128)(2,1)S(1)}, bf16[128,400]{1,0:T(8,128)(2,1)}, u32[]{:S(2)}, u32[]{:S(2)}) collective-permute-start(bf16[128,400]{1,0:T(8,128)(2,1)S(1)} %get-tuple-element.510), channel_id=1, source_target_pairs={{0,4},{4,8},{8,12},{12,16},{16,20},{20,24},{24,28},{28,32},{32,36}... | collective-permute-start | bytes 307208 | tf_op jit(solution)/shard_map/ppermute | solution.py:24
  765.7 4.4 copy-start.23
  765.7 155.2 %copy-start.21 = (f32[256]{0:T(256)S(1)}, f32[256]{0:T(256)}, u32[]{:S(2)}) copy-start(f32[256]{0:T(256)} %param.45) | copy-start | bytes 3076
  769.2 0.8 copy-start.2
  (1 other events, 0.8 us)
Sparse Core Ops, SparseCore 0:
  770.2 149.5 all-reduce.1
where the time goes:
time: 932 us; the launch traced here: 930 us
  blocking collectives  601 us (64%)
  waiting for transfers between devices  199 us (21%)
  local copies, waits for them, and re-layouts  39.8 us (4%)
  starting transfers between devices  32.5 us (3%)
  other arithmetic  26.4 us (3%)
  between operations  16.1 us (2%)
  matrix products  15.7 us (2%)
    psum x1, blocking collectives, body(): total_rel = lax.psum(rel_grad, 'dom')  601 us
    psum x1, waiting for transfers between devices, body(): full_grad = lax.psum(whole_grad, 'rel')  149 us
    ppermute x4, waiting for transfers between devices, from_partner(): return lax.ppermute(block, axis, route)  49.5 us
    ppermute x4, starting transfers between devices, from_partner(): return lax.ppermute(block, axis, route)  19.6 us
  transfers between devices with their start and end apart: 9, of which 5 were waited for; matrix products, arithmetic and copies ran while one was open for 6% of the time, Pallas kernels for 0%

commit v1 on v0

--- a/solution.py
+++ b/solution.py
@@ -194,7 +194,8 @@
         / jnp.sqrt(rel_state + jnp.mean(total_rel * total_rel, axis=1))[:, None]
     )
     whole_grad = local + return_block(far_grad, mask)
-    full_grad = lax.psum(whole_grad, "rel")
+    blocks = lax.all_gather(whole_grad, "rel")
+    full_grad = jnp.sum(blocks, axis=0)
     emb_new, state_new = adagrad(emb, emb_state, full_grad)
     return (emb_new, state_new, rel_new)
 

time: 932 us -> 897 us (0.962)
  the two profiles are of different devices: /device:TPU:1 before, /device:TPU:8 now
where the time goes in v1:
time: 897 us; the launch traced here: 896 us
  blocking collectives  711 us (79%)
  waiting for transfers between devices  51.9 us (6%)
  local copies, waits for them, and re-layouts  42.5 us (5%)
  starting transfers between devices  30.3 us (3%)
  other arithmetic  28.8 us (3%)
  between operations  16 us (2%)
  matrix products  15.7 us (2%)
    psum x1, blocking collectives, body(): total_rel = lax.psum(rel_grad, 'dom')  711 us
    ppermute x4, waiting for transfers between devices, from_partner(): return lax.ppermute(block, axis, route)  51.9 us
  transfers between devices with their start and end apart: 9, of which 4 were waited for; matrix products, arithmetic and copies ran while one was open for 6% of the time, Pallas kernels for 0%

profile of v1, /device:TPU:8, one launch (start us, length us, event | category | flops | bytes accessed | tf_op | source)
XLA Modules:
  0.0 896.2 jit_solution(9574803074429486654)
XLA Ops:
  11.7 5.2 collective-permute-start.14
  18.4 9.7 %conditional.14 = (bf16[256,400]{1,0:T(8,128)(2,1)}) conditional(s32[]{:T(128)} %convert_element_type.168, bf16[256,400]{1,0:T(8,128)(2,1)S(1)} %convert_element_type.169, bf16[256,400]{1,0:T(8,128)(2,1)S(1)} %convert_element_type.169), branch_computations={%region_0.1_spmd, %region_1.2_spmd} | conditional | bytes 819248 | solution.py:60
  18.4 3.2 collective-permute-start
  21.6 6.5 collective-permute-done
  28.2 1.6 gather_fusion.2
  30.9 17.8 %conditional.15 = (bf16[256,400]{1,0:T(8,128)(2,1)}) conditional(s32[]{:T(128)} %convert_element_type.167, bf16[256,400]{1,0:T(8,128)(2,1)} %get-tuple-element.686, bf16[256,400]{1,0:T(8,128)(2,1)} %get-tuple-element.686), branch_computations={%region_2.3_spmd, %region_3.4_spmd} | conditional | bytes 1228848 | solution.py:60
  30.9 5.9 collective-permute-start.1
  36.8 11.2 %collective-permute-done.1 = bf16[256,400]{1,0:T(8,128)(2,1)S(1)} collective-permute-done((bf16[256,400]{1,0:T(8,128)(2,1)}, bf16[256,400]{1,0:T(8,128)(2,1)S(1)}, u32[]{:S(2)}, u32[]{:S(2)}) %collective-permute-start.1) | collective-permute-done | bytes 204832 | tf_op jit(solution)/shard_map/cond/branch_1_fun/ppermute | solution.py:16
  48.7 3.0 gather_fusion.3
  57.4 33.8 %while.21 = (s32[]{:T(128)}, f32[256,400]{1,0:T(8,128)S(1)}, f32[256,400]{1,0:T(8,128)S(1)}, f32[1024,400]{0,1:T(8,128)}, f32[8,400]{1,0:T(8,128)S(1)}, /*index=...) while((s32[]{:T(128)}, f32[256,400]{1,0:T(8,128)S(1)}, ...), condition=%wide.region_18.19_spmd, body=%wide.region_15.18_spmd.sunk | while | flops 1283260032 | bytes 38448668 | solution.py:155
  59.5 2.3 gather_fusion
  64.9 2.0 multiply_convert_fusion.3
  66.9 3.6 gather_fusion.1
  70.6 2.0 copy.105
  72.5 3.5 bitcast_multiply_fusion.6
  77.5 3.8 scatter_fusion
  82.8 3.8 scatter_fusion.1
  86.6 3.7 convolution_add_fusion.7
  98.5 1.9 gather_fusion.6
  108.0 2.0 copy.71
  110.0 3.4 scatter_custom_fusion.3
  115.7 5.2 collective-permute-start.16
  121.8 15.3 %conditional.21 = (f32[256,400]{1,0:T(8,128)}) conditional(s32[]{:T(128)} %convert_element_type.168, f32[256,400]{1,0:T(8,128)} %bitcast_add_fusion, f32[256,400]{1,0:T(8,128)} %bitcast_add_fusion), branch_computations={%region_19.20_spmd, %region_20.21_spmd} | conditional | bytes 2457648 | solution.py:71
  121.8 2.1 collective-permute-start.7
  123.9 12.4 %collective-permute-done.7 = f32[256,400]{1,0:T(8,128)S(1)} collective-permute-done((f32[256,400]{1,0:T(8,128)}, f32[256,400]{1,0:T(8,128)S(1)}, u32[]{:S(2)}, u32[]{:S(2)}) %collective-permute-start.7) | collective-permute-done | bytes 409632 | tf_op jit(solution)/shard_map/cond/branch_1_fun/ppermute | solution.py:16
  137.1 28.7 %conditional.22 = (f32[256,400]{1,0:T(8,128)}) conditional(s32[]{:T(128)} %convert_element_type.167, f32[256,400]{1,0:T(8,128)} %get-tuple-element.693, f32[256,400]{1,0:T(8,128)} %get-tuple-element.693), branch_computations={%region_21.22_spmd, %region_22.23_spmd} | conditional | bytes 2457648 | solution.py:71
  137.1 6.1 collective-permute-start.8
  143.2 21.8 %collective-permute-done.8 = f32[256,400]{1,0:T(8,128)S(1)} collective-permute-done((f32[256,400]{1,0:T(8,128)}, f32[256,400]{1,0:T(8,128)S(1)}, u32[]{:S(2)}, u32[]{:S(2)}) %collective-permute-start.8) | collective-permute-done | bytes 409632 | tf_op jit(solution)/shard_map/cond/branch_1_fun/ppermute | solution.py:16
  167.1 2.3 scatter_fusion.2
  170.6 2.3 scatter_custom_fusion.4
  174.2 710.7 %psum.7 = f32[8,400]{1,0:T(8,128)S(1)} all-reduce(f32[8,400]{1,0:T(8,128)S(1)} %convolution_add_fusion.4), channel_id=1, replica_groups=mesh['dom'=128,'rel'=4] {'dom'}, use_global_device_ids=true, to_apply=%region_39.40 | all-reduce | flops 3200 | bytes 25600 | tf_op jit(solution)/shard_map/psum | solution.py:189
  885.7 1.9 reduce_sum.47
  (134 shorter events, 46.4 us)
Async XLA Ops:
  7.2 1.3 copy-start.15
  7.2 878.5 %all-gather.3.cloned.1.call-start = ((), (), s32[]{:S(2)}) async-start(), calls=%async_computation | async-start | bytes 2621440 | tf_op jit(solution)/shard_map/all_gather | solution.py:197
  8.5 19.6 %copy-start.11 = (s32[1,512]{1,0:T(1,128)S(1)}, s32[1,512]{1,0:T(1,128)}, u32[]{:S(2)}) copy-start(s32[1,512]{1,0:T(1,128)} %param.50) | copy-start | bytes 6148
  8.5 19.6 %copy-start.10 = (s32[1,512]{1,0:T(1,128)S(1)}, s32[1,512]{1,0:T(1,128)}, u32[]{:S(2)}) copy-start(s32[1,512]{1,0:T(1,128)} %param.49) | copy-start | bytes 6148
  10.4 87.0 %collective-permute-start.15 = (bf16[128,400]{1,0:T(8,128)(2,1)}, bf16[128,400]{1,0:T(8,128)(2,1)}, u32[]{:S(2)}, u32[]{:S(2)}) collective-permute-start(bf16[128,400]{1,0:T(8,128)(2,1)} %get-tuple-element.528), channel_id=1, source_target_pairs={{4,0},{8,4},{12,8},{16,12},{20,16},{24,20},{28,24},{32,28},{36,32}... | collective-permute-start | bytes 307208 | tf_op jit(solution)/shard_map/ppermute | solution.py:27
  11.7 85.7 %collective-permute-start.14 = (bf16[128,400]{1,0:T(8,128)(2,1)}, bf16[128,400]{1,0:T(8,128)(2,1)}, u32[]{:S(2)}, u32[]{:S(2)}) collective-permute-start(bf16[128,400]{1,0:T(8,128)(2,1)} %get-tuple-element.527), channel_id=1, source_target_pairs={{0,4},{4,8},{8,12},{12,16},{16,20},{20,24},{24,28},{28,32},{32,36}... | collective-permute-start | bytes 307208 | tf_op jit(solution)/shard_map/ppermute | solution.py:24
  18.4 9.7 %collective-permute-start = (bf16[256,400]{1,0:T(8,128)(2,1)S(1)}, bf16[256,400]{1,0:T(8,128)(2,1)}, u32[]{:S(2)}, u32[]{:S(2)}) collective-permute-start(bf16[256,400]{1,0:T(8,128)(2,1)S(1)} %param.1), channel_id=1, source_target_pairs={{0,4},{4,0},{8,12},{12,8},{16,20},{20,16},{24,28},{28,24},{32,36},... | collective-permute-start | bytes 614408 | tf_op jit(solution)/shard_map/cond/branch_1_fun/ppermute | solution.py:16
  28.2 1.7 copy-start.12
  28.2 1.7 copy-start.13
  30.9 17.1 %collective-permute-start.1 = (bf16[256,400]{1,0:T(8,128)(2,1)}, bf16[256,400]{1,0:T(8,128)(2,1)S(1)}, u32[]{:S(2)}, u32[]{:S(2)}) collective-permute-start(bf16[256,400]{1,0:T(8,128)(2,1)} %param.3), channel_id=1, source_target_pairs={{0,8},{8,0},{4,12},{12,4},{16,24},{24,16},{20,28},{28,20},{32,40},... | collective-permute-start | bytes 614408 | tf_op jit(solution)/shard_map/cond/branch_1_fun/ppermute | solution.py:16
  51.7 1.4 copy-start.14
  53.5 0.9 copy-start.5
  57.4 33.8 %copy-start.16 = (s32[1,256]{1,0:T(1,128)S(1)}, s32[1,256]{1,0:T(1,128)}, u32[]{:S(2)}) copy-start(s32[1,256]{1,0:T(1,128)} %param.56) | copy-start | bytes 3076
  57.4 33.8 %copy-start.17 = (s32[1,256]{1,0:T(1,128)S(1)}, s32[1,256]{1,0:T(1,128)}, u32[]{:S(2)}) copy-start(s32[1,256]{1,0:T(1,128)} %param.55) | copy-start | bytes 3076
  63.4 1.5 copy-start.4
  64.5 2.4 copy-start.3
  86.6 3.8 copy-start
  91.3 1.9 copy-start.19
  92.3 3.8 copy-start.6
  98.5 3.5 copy-start.7
  101.4 1.0 copy-start.8
  102.5 2.0 copy-start.1
  114.4 55.0 %collective-permute-start.17 = (bf16[128,400]{1,0:T(8,128)(2,1)S(1)}, bf16[128,400]{1,0:T(8,128)(2,1)}, u32[]{:S(2)}, u32[]{:S(2)}) collective-permute-start(bf16[128,400]{1,0:T(8,128)(2,1)S(1)} %get-tuple-element.526), channel_id=1, source_target_pairs={{4,0},{8,4},{12,8},{16,12},{20,16},{24,20},{28,24},{32,28},{36,32}... | collective-permute-start | bytes 307208 | tf_op jit(solution)/shard_map/ppermute | solution.py:27
  115.7 53.7 %collective-permute-start.16 = (bf16[128,400]{1,0:T(8,128)(2,1)S(1)}, bf16[128,400]{1,0:T(8,128)(2,1)}, u32[]{:S(2)}, u32[]{:S(2)}) collective-permute-start(bf16[128,400]{1,0:T(8,128)(2,1)S(1)} %get-tuple-element.525), channel_id=1, source_target_pairs={{0,4},{4,8},{8,12},{12,16},{16,20},{20,24},{24,28},{28,32},{32,36}... | collective-permute-start | bytes 307208 | tf_op jit(solution)/shard_map/ppermute | solution.py:24
  121.8 14.5 %collective-permute-start.7 = (f32[256,400]{1,0:T(8,128)}, f32[256,400]{1,0:T(8,128)S(1)}, u32[]{:S(2)}, u32[]{:S(2)}) collective-permute-start(f32[256,400]{1,0:T(8,128)} %param.17), channel_id=1, source_target_pairs={{0,4},{4,0},{8,12},{12,8},{16,20},{20,16},{24,28},{28,24},{32,36},... | collective-permute-start | bytes 1228808 | tf_op jit(solution)/shard_map/cond/branch_1_fun/ppermute | solution.py:16
  137.1 27.9 %collective-permute-start.8 = (f32[256,400]{1,0:T(8,128)}, f32[256,400]{1,0:T(8,128)S(1)}, u32[]{:S(2)}, u32[]{:S(2)}) collective-permute-start(f32[256,400]{1,0:T(8,128)} %param.19), channel_id=1, source_target_pairs={{0,8},{8,0},{4,12},{12,4},{16,24},{24,16},{20,28},{28,20},{32,40},... | collective-permute-start | bytes 1228808 | tf_op jit(solution)/shard_map/cond/branch_1_fun/ppermute | solution.py:16
  169.4 4.4 copy-start.9
  169.4 715.5 %copy-start.20 = (f32[8]{0:T(128)S(1)}, f32[8]{0:T(128)}, u32[]{:S(2)}) copy-start(f32[8]{0:T(128)} %param.47) | copy-start | bytes 100
  172.9 0.8 copy-start.2
  174.2 713.5 %copy-start.18 = (f32[256]{0:T(256)S(1)}, f32[256]{0:T(256)}, u32[]{:S(2)}) copy-start(f32[256]{0:T(256)} %param.45) | copy-start | bytes 3076
Sparse Core Ops, SparseCore 0:
  173.9 40.7 all-gather.2
